TPU v7x, 32 devices: a whole 2x2x4 slice. The times are simulated.
32 devices in a mesh: modes: 16 (over z, x, core), gz: 2 (over y).
Axes of the slice: x: 2, y: 2, z: 4, core: 2. Of those that a mesh axis runs over, the one named last changes fastest.
Arguments:
- fields: float32 [288, 64, 4, 128], P('modes', None, 'gz'), may hold values from -6 to 6
- mean_coeff: float32 [64, 4, 128], P(None, 'gz'), may hold values from 0.5 to 4
- random_coeff: float32 [10, 64, 4, 128], P(None, None, 'gz'), may hold values from -2.5 to 2.5
- coupling: int32 [1606, 4], replicated, may hold values from 0 to 285, as said below
- mode_slots: int32 [286], replicated, may hold values from 0 to 287, as said below
Outputs:
- applied: float32 [288, 64, 4, 128], P('modes', None, 'gz')
Inputs may be any that keep to these rules, and one draw needn't show every extreme that they name: `coupling`: each row couples a mode with itself under term 0, or a mode with the mode one higher in the degree of one variable under the term that belongs to that variable, in both orders; each of the 10 variables belongs to a different term of 1 to 10, in no particular assignment; every such pair appears exactly once, in no particular order; modes are numbered by total degree. `mode_slots`: the slots are distinct.
All inputs are finite; a program needn't handle non-finite values.
Results may differ from a plain program's by a relative error of at most 0.000082.
Values sent between devices are 32-bit elements; how exact they have to be, the bound alone decides.
A program may use at most 64 MiB of HBM per device.

v0:
```python
import functools

import jax
import jax.numpy as jnp
from jax import lax
from jax.experimental import pallas as pl
from jax.experimental.pallas import tpu as pltpu
from jax.sharding import PartitionSpec as P

ACCS = 4
UNROLL = 8


def turn(value, shift, axis):
    size = value.shape[axis]
    shift %= size
    if shift == 0:
        return value
    low = lax.slice_in_dim(value, size - shift, size, axis=axis)
    high = lax.slice_in_dim(value, 0, size - shift, axis=axis)
    return jnp.concatenate([low, high], axis=axis)


def send_order(count):
    half = count // 2
    return sorted(range(1, count), key=lambda d: (abs(d - half), d))


def groups(own, parts):
    per = -(-own // parts)
    return per, [min(j * per, own - per) for j in range(parts)]


def barrier_with_peers(peers_modes, peers_gz):
    me, layer = lax.axis_index("modes"), lax.axis_index("gz")
    barrier = pltpu.get_barrier_semaphore()

    @pl.loop(1, peers_modes)
    def _(step):
        pl.semaphore_signal(
            barrier, inc=1, device_id=(lax.rem(me + step, peers_modes), layer),
            device_id_type=pl.DeviceIdType.MESH)

    @pl.loop(1, peers_gz)
    def _(step):
        pl.semaphore_signal(
            barrier, inc=1, device_id=(me, lax.rem(layer + step, peers_gz)),
            device_id_type=pl.DeviceIdType.MESH)

    pl.semaphore_wait(barrier, peers_modes + peers_gz - 2)


def spread_kernel(n, g, rows, depth, fields, coef, main, ylo, yhi, zlo, zhi, clo, chi,
                  ylo_out, yhi_out, zlo_out, zhi_out,
                  own_sem, send_sem, recv_sem, halo_send, halo_recv, coef_send, coef_recv):
    me, layer = lax.axis_index("modes"), lax.axis_index("gz")
    own = fields.shape[0]
    lines = rows * depth
    mesh_id = pl.DeviceIdType.MESH
    has = (me > 0, me < n - 1, layer > 0, layer < g - 1)
    to = ((me - 1, layer), (me + 1, layer), (me, layer - 1), (me, layer + 1))
    packed = (ylo_out, yhi_out, zlo_out, zhi_out)
    landing = (yhi, ylo, zhi, zlo)
    barrier_with_peers(n, g)

    def block_copy(step):
        target = lax.rem(me + step, n)
        return pltpu.make_async_remote_copy(
            src_ref=fields.at[:, target], dst_ref=main.at[me],
            send_sem=send_sem.at[step], recv_sem=recv_sem.at[step],
            device_id=(target, layer), device_id_type=mesh_id)

    def coef_copy(side):
        return pltpu.make_async_remote_copy(
            src_ref=coef, dst_ref=(chi, clo)[side - 2],
            send_sem=coef_send.at[side - 2], recv_sem=coef_recv.at[side - 2],
            device_id=to[side], device_id_type=mesh_id)

    def halo_copy(side, source):
        return pltpu.make_async_remote_copy(
            src_ref=packed[side].at[source], dst_ref=landing[side].at[source],
            send_sem=halo_send.at[side, source], recv_sem=halo_recv.at[side, source],
            device_id=to[side], device_id_type=mesh_id)

    order = send_order(n)
    for step in order:
        block_copy(step).start()
    mine = pltpu.make_async_copy(fields.at[:, me], main.at[me], own_sem)
    mine.start()
    for side in (2, 3):
        @pl.when(has[side])
        def _():
            coef_copy(side).start()

    y_per, y_starts = groups(own, rows)
    z_per, z_starts = groups(own, depth)

    def pack(source):
        line = lax.broadcasted_iota(jnp.int32, (1, lines, 1), 1)
        for out, edge in ((ylo_out, 0), (yhi_out, rows - 1)):
            tile = None
            for j, start in enumerate(y_starts):
                part = turn(main[source, start:start + y_per], (j - edge) * depth, 1)
                tile = part if tile is None else jnp.where(line // depth == j, part, tile)
            out[source] = tile
        for out, edge in ((zlo_out, 0), (zhi_out, depth - 1)):
            tile = None
            for j, start in enumerate(z_starts):
                part = turn(main[source, start:start + z_per], j - edge, 1)
                tile = part if tile is None else jnp.where(line % depth == j, part, tile)
            out[source] = tile

    def send_halo(source):
        for side in range(4):
            @pl.when(has[side])
            def _():
                halo_copy(side, source).start()

    mine.wait()
    pack(me)
    previous = me
    for step in order:
        source = lax.rem(me + n - step, n)
        block_copy(step).wait_recv()
        send_halo(previous)
        pack(source)
        previous = source
    for step in order:
        block_copy(step).wait_send()
    send_halo(previous)
    for side in range(4):
        @pl.when(has[side])
        def _():
            @pl.loop(0, n)
            def _(source):
                halo_copy(side, source).wait_send()

        opposite = (1, 0, 3, 2)[side]

        @pl.when(has[opposite])
        def _():
            @pl.loop(0, n)
            def _(source):
                halo_copy(side, source).wait_recv()
    for side in (2, 3):
        @pl.when(has[side])
        def _():
            coef_copy(side).wait_send()

        @pl.when(has[5 - side])
        def _():
            coef_copy(side).wait_recv()


def mix_kernel(n, g, rows, depth, pairs, couple, weight, slots, main, ylo, yhi, zlo, zhi,
               coef, clo, chi, out, shifted, faces, acc):
    me, layer = lax.axis_index("modes"), lax.axis_index("gz")
    own = main.shape[1]
    lines = rows * depth
    lanes = main.shape[3]
    terms = coef.shape[0]
    line = lax.broadcasted_iota(jnp.int32, (1, lines, lanes), 1)
    lane = lax.broadcasted_iota(jnp.int32, (1, lines, lanes), 2)
    row, deep = line // depth, line % depth

    def x_shift(value, offset):
        moved = pltpu.roll(value, offset % lanes, 2)
        edge = 0 if offset == 1 else lanes - 1
        return jnp.where(lane == edge, 0.0, moved)

    centre = coef[:, depth:depth + lines, :]
    before, after = clo[:, depth:depth + lines, :], chi[:, depth:depth + lines, :]
    z_before = jnp.where(layer > 0, turn(before, 1 - depth, 1), 0.0)
    z_after = jnp.where(layer < g - 1, turn(after, depth - 1, 1), 0.0)
    around = (
        coef[:, 0:lines, :],
        coef[:, 2 * depth:2 * depth + lines, :],
        jnp.where(deep == 0, z_before, turn(centre, 1, 1)),
        jnp.where(deep == depth - 1, z_after, turn(centre, -1, 1)),
        x_shift(centre, 1),
        x_shift(centre, -1),
    )
    total = None
    for m, other in enumerate(around):
        face = 0.5 * (centre + other)
        faces[:, m + 1] = face
        total = face if total is None else total + face
    faces[:, 0] = total

    y_per, y_starts = groups(own, rows)
    z_per, z_starts = groups(own, depth)

    def spans(starts, per):
        seen = 0
        for j, start in enumerate(starts):
            yield j, seen, min(own, start + per), start
            seen = min(own, start + per)

    has = (me > 0, me < n - 1, layer > 0, layer < g - 1)

    @pl.loop(0, n)
    def _(source):
        base = source * own
        value = main[source]
        shifted[pl.ds(base, own), 0] = value
        shifted[pl.ds(base, own), 5] = x_shift(value, 1)
        shifted[pl.ds(base, own), 6] = x_shift(value, -1)

        def edge_pieces(ref, starts, per, wanted, unit, here):
            pieces = []
            for j, first, stop, start in spans(starts, per):
                if stop > first:
                    tile = ref[source, first - start:stop - start]
                    pieces.append(turn(tile, (wanted - j) * unit, 1))
            joined = pieces[0] if len(pieces) == 1 else jnp.concatenate(pieces, axis=0)
            return jnp.where(here, joined, 0.0)

        low = edge_pieces(ylo, y_starts, y_per, 0, depth, has[0])
        high = edge_pieces(yhi, y_starts, y_per, rows - 1, depth, has[1])
        shifted[pl.ds(base, own), 1] = jnp.where(row == 0, low, turn(value, depth, 1))
        shifted[pl.ds(base, own), 2] = jnp.where(row == rows - 1, high, turn(value, -depth, 1))
        near = edge_pieces(zlo, z_starts, z_per, 0, 1, has[2])
        far = edge_pieces(zhi, z_starts, z_per, depth - 1, 1, has[3])
        shifted[pl.ds(base, own), 3] = jnp.where(deep == 0, near, turn(value, 1, 1))
        shifted[pl.ds(base, own), 4] = jnp.where(deep == depth - 1, far, turn(value, -1, 1))
        for a in range(ACCS):
            acc[a, pl.ds(base, own)] = jnp.zeros_like(value)

    def add_row(p, a):
        target = slots[couple[p]]
        source = slots[couple[pairs + p]]
        term = couple[2 * pairs + p]
        image = faces[term, 0] * shifted[source, 0]
        first = faces[term, 1] * shifted[source, 1] + faces[term, 2] * shifted[source, 2]
        second = faces[term, 3] * shifted[source, 3] + faces[term, 4] * shifted[source, 4]
        third = faces[term, 5] * shifted[source, 5] + faces[term, 6] * shifted[source, 6]
        image = (image - first) - (second + third)
        acc[a, target] = acc[a, target] + weight[p] * image

    whole = pairs // UNROLL

    @pl.loop(0, whole)
    def _(block):
        for u in range(UNROLL):
            add_row(block * UNROLL + u, u % ACCS)

    for p in range(whole * UNROLL, pairs):
        add_row(p, p % ACCS)

    @pl.loop(0, n)
    def _(source):
        base = source * own
        result = acc[0, pl.ds(base, own)]
        for a in range(1, ACCS):
            result = result + acc[a, pl.ds(base, own)]
        out[source] = result


def collect_kernel(n, result, out, own_sem, send_sem, recv_sem):
    me, layer = lax.axis_index("modes"), lax.axis_index("gz")
    barrier_with_peers(n, 1)

    def block_copy(step):
        target = lax.rem(me + step, n)
        return pltpu.make_async_remote_copy(
            src_ref=result.at[target], dst_ref=out.at[:, me],
            send_sem=send_sem.at[step], recv_sem=recv_sem.at[step],
            device_id=(target, layer), device_id_type=pl.DeviceIdType.MESH)

    order = send_order(n)
    for step in order:
        block_copy(step).start()
    mine = pltpu.make_async_copy(result.at[me], out.at[:, me], own_sem)
    mine.start()
    mine.wait()
    for step in order:
        block_copy(step).wait_recv()
    for step in order:
        block_copy(step).wait_send()


def body(fields, mean_coeff, random_coeff, coupling, mode_slots):
    n, g = lax.axis_size("modes"), lax.axis_size("gz")
    own, row_total, depth, across = fields.shape
    rows = row_total // n
    lines = rows * depth
    f32 = jnp.float32
    vmem = pl.BlockSpec(memory_space=pltpu.VMEM)
    smem = pl.BlockSpec(memory_space=pltpu.SMEM)
    dma = pltpu.SemaphoreType.DMA

    coef = jnp.concatenate([mean_coeff[None], random_coeff], axis=0)
    coef = jnp.pad(coef, ((0, 0), (1, 1), (0, 0), (0, 0)))
    coef = lax.dynamic_slice_in_dim(coef, lax.axis_index("modes") * rows, rows + 2, 1)
    terms = coef.shape[0]
    coef = coef.reshape(terms, (rows + 2) * depth, across)

    degree = coupling[:, 3].astype(f32)
    raw = (degree + 1.0) / jnp.sqrt((2.0 * degree + 1.0) * (2.0 * degree + 3.0))
    weight = jnp.where(coupling[:, 2] == 0, jnp.ones_like(raw), raw)
    pairs = coupling.shape[0]
    couple = coupling[:, :3].T.reshape(-1)

    y_per, _ = groups(own, rows)
    z_per, _ = groups(own, depth)
    block = jax.ShapeDtypeStruct((n, own, lines, across), f32)
    y_pack = jax.ShapeDtypeStruct((n, y_per, lines, across), f32)
    z_pack = jax.ShapeDtypeStruct((n, z_per, lines, across), f32)
    coef_like = jax.ShapeDtypeStruct(coef.shape, f32)
    spread = pl.pallas_call(
        functools.partial(spread_kernel, n, g, rows, depth),
        out_shape=(block, y_pack, y_pack, z_pack, z_pack, coef_like, coef_like),
        in_specs=[vmem, vmem],
        out_specs=[vmem] * 7,
        scratch_shapes=[
            pltpu.VMEM(y_pack.shape, f32), pltpu.VMEM(y_pack.shape, f32),
            pltpu.VMEM(z_pack.shape, f32), pltpu.VMEM(z_pack.shape, f32),
            dma, dma((n,)), dma((n,)), dma((4, n)), dma((4, n)), dma((2,)), dma((2,)),
        ],
        compiler_params=pltpu.CompilerParams(collective_id=0, has_side_effects=True),
        name="spread",
    )
    main, ylo, yhi, zlo, zhi, clo, chi = spread(fields.reshape(own, n, lines, across), coef)

    mix = pl.pallas_call(
        functools.partial(mix_kernel, n, g, rows, depth, pairs),
        out_shape=block,
        in_specs=[smem, smem, smem] + [vmem] * 8,
        out_specs=vmem,
        scratch_shapes=[
            pltpu.VMEM((n * own, 7, lines, across), f32),
            pltpu.VMEM((terms, 7, lines, across), f32),
            pltpu.VMEM((ACCS, n * own, lines, across), f32),
        ],
        name="mix",
    )
    result = mix(couple, weight, mode_slots, main, ylo, yhi, zlo, zhi, coef, clo, chi)

    collect = pl.pallas_call(
        functools.partial(collect_kernel, n),
        out_shape=jax.ShapeDtypeStruct((own, n, lines, across), f32),
        in_specs=[vmem],
        out_specs=vmem,
        scratch_shapes=[dma, dma((n,)), dma((n,))],
        compiler_params=pltpu.CompilerParams(collective_id=1, has_side_effects=True),
        name="collect",
    )
    return collect(result).reshape(fields.shape)


def solution(mesh):
    in_specs = (
        P("modes", None, "gz", None),
        P(None, "gz", None),
        P(None, None, "gz", None),
        P(),
        P(),
    )
    out_specs = P("modes", None, "gz", None)
    return jax.shard_map(body, mesh=mesh, in_specs=in_specs, out_specs=out_specs, check_vma=False)
```

profile of v0, /device:TPU:9, one launch (start us, length us, event | category | flops | bytes accessed | tf_op | source)
XLA Modules:
  0.0 96.1 jit_solution(9664785269350322070)
XLA Ops:
  0.0 1.5 %fusion.3.weight = f32[1606]{0:T(1024)} fusion(s32[1606,4]{0,1:T(4,128)} %param.8), kind=kLoop, calls=%fused_computation.8 | loop fusion | flops 14454 | bytes 19272 | tf_op jit(solution)/shard_map/jit(_where)/select_n | solution.py:300
  1.5 0.7 slice_bitcast_fusion
  2.2 0.7 reshape.24.couple
  2.9 0.9 fusion.1
  3.8 0.7 reshape.26.coef
  4.5 43.6 %spread.1 = (f32[16,18,8,128]{3,2,1,0:T(8,128)}, f32[16,5,8,128]{3,2,1,0:T(8,128)}, f32[16,5,8,128]{3,2,1,0:T(8,128)}, f32[16,9,8,128]{3,2,1,0:T(8,128)}, f32[16...) custom-call(f32[18,16,8,128]{3,2,1,0:T(8,128)} %bitcast.6, f32[11,12,128]{2,1,0:T(8,128)} %reshape.26.coef), custom_call_target="tpu_custom_call" | custom-call | tf_op jit(solution)/shard_map/spread/pallas_call | solution.py:323
  48.1 16.0 %mix.1.result = f32[16,18,8,128]{3,2,1,0:T(8,128)} custom-call(s32[4818]{0:T(1024)} %reshape.24.couple, f32[1606]{0:T(1024)} %fusion.3.weight, s32[286]{0:T(512)} %slots.1, f32[16,18,8,128]{3,2,1,0:T(8,128)} %get-tuple-element.12.main, f32[16,5,8,128]{3,2,1,0:T(8,128)} %get-tuple-element.13.ylo, f32[16,5,8,128]{3,2,1,0:T(8,128)} %get-tuple-element.14.yhi, ...), custom_call_target="tpu_custom_call" | custom-call | tf_op jit(solution)/shard_map/mix/pallas_call | solution.py:337
  64.0 29.7 %collect.1 = f32[18,16,8,128]{3,2,1,0:T(8,128)} custom-call(f32[16,18,8,128]{3,2,1,0:T(8,128)} %mix.1.result), custom_call_target="tpu_custom_call" | custom-call | tf_op jit(solution)/shard_map/collect/pallas_call | solution.py:348
  93.7 2.4 %copy.7 = f32[18,64,2,128]{3,2,1,0:T(2,128)} copy(f32[18,64,2,128]{3,2,1,0:T(2,128)} %bitcast.5) | data formatting | bytes 2359296
where the time goes:
time: 97.8 us; the launch traced here: 96.1 us
  Pallas kernels  89.2 us (91%)
  local copies, waits for them, and re-layouts  4.5 us (5%)
  other arithmetic  2.35 us (2%)
    pallas_call x1, Pallas kernels, body(): spread(fields.reshape(own, n, lines, across), coef)  43.6 us
    pallas_call x1, Pallas kernels, body(): return collect(result).reshape(fields.shape)  29.7 us
    pallas_call x1, Pallas kernels, body(): mix(couple, weight, mode_slots, main, ylo, yhi, zlo, zhi, coef, clo, chi)  16 us
    unnamed x1, local copies, waits for them, and re-layouts  2.39 us

commit v1 on v0

--- a/solution.py
+++ b/solution.py
@@ -8,7 +8,7 @@
 from jax.sharding import PartitionSpec as P
 
 ACCS = 4
-UNROLL = 8
+UNROLL = 22
 
 
 def turn(value, shift, axis):
@@ -22,8 +22,7 @@
 
 
 def send_order(count):
-    half = count // 2
-    return sorted(range(1, count), key=lambda d: (abs(d - half), d))
+    return sorted(range(1, count), key=lambda d: (min(d, count - d), d))
 
 
 def groups(own, parts):
@@ -50,7 +49,8 @@
     pl.semaphore_wait(barrier, peers_modes + peers_gz - 2)
 
 
-def spread_kernel(n, g, rows, depth, fields, coef, main, ylo, yhi, zlo, zhi, clo, chi,
+def spread_kernel(n, g, rows, depth, couple, slots, table, fields, coef,
+                  main, ylo, yhi, zlo, zhi, clo, chi, to_off, from_off, term_off, weight,
                   ylo_out, yhi_out, zlo_out, zhi_out,
                   own_sem, send_sem, recv_sem, halo_send, halo_recv, coef_send, coef_recv):
     me, layer = lax.axis_index("modes"), lax.axis_index("gz")
@@ -94,6 +94,18 @@
 
     y_per, y_starts = groups(own, rows)
     z_per, z_starts = groups(own, depth)
+
+    pairs = couple.shape[1]
+    share = -(-pairs // n)
+
+    def decode(part):
+        @pl.loop(part * share, min(pairs, (part + 1) * share))
+        def _(p):
+            term = couple[2, p]
+            to_off[p] = slots[couple[0, p]] * lines
+            from_off[p] = slots[couple[1, p]] * (7 * lines)
+            term_off[p] = term * (7 * lines)
+            weight[p] = jnp.where(term == 0, jnp.float32(1.0), table[couple[3, p]])
 
     def pack(source):
         line = lax.broadcasted_iota(jnp.int32, (1, lines, 1), 1)
@@ -116,14 +128,16 @@
             def _():
                 halo_copy(side, source).start()
 
+    decode(0)
     mine.wait()
     pack(me)
     previous = me
-    for step in order:
+    for part, step in enumerate(order):
         source = lax.rem(me + n - step, n)
         block_copy(step).wait_recv()
         send_halo(previous)
         pack(source)
+        decode(part + 1)
         previous = source
     for step in order:
         block_copy(step).wait_send()
@@ -152,7 +166,7 @@
             coef_copy(side).wait_recv()
 
 
-def mix_kernel(n, g, rows, depth, pairs, couple, weight, slots, main, ylo, yhi, zlo, zhi,
+def mix_kernel(n, g, rows, depth, pairs, to_off, from_off, term_off, weight, main, ylo, yhi, zlo, zhi,
                coef, clo, chi, out, shifted, faces, acc):
     me, layer = lax.axis_index("modes"), lax.axis_index("gz")
     own = main.shape[1]
@@ -180,12 +194,17 @@
         x_shift(centre, 1),
         x_shift(centre, -1),
     )
+
+    def put_faces(m, value):
+        for k in range(terms):
+            faces[(k * 7 + m) * lines:(k * 7 + m + 1) * lines, :] = value[k]
+
     total = None
     for m, other in enumerate(around):
         face = 0.5 * (centre + other)
-        faces[:, m + 1] = face
+        put_faces(m + 1, face)
         total = face if total is None else total + face
-    faces[:, 0] = total
+    put_faces(0, total)
 
     y_per, y_starts = groups(own, rows)
     z_per, z_starts = groups(own, depth)
@@ -198,13 +217,18 @@
 
     has = (me > 0, me < n - 1, layer > 0, layer < g - 1)
 
+    def put(base, m, value):
+        for i in range(own):
+            start = pl.multiple_of(base * (7 * lines), lines) + (i * 7 + m) * lines
+            shifted[pl.ds(start, lines), :] = value[i]
+
     @pl.loop(0, n)
     def _(source):
         base = source * own
         value = main[source]
-        shifted[pl.ds(base, own), 0] = value
-        shifted[pl.ds(base, own), 5] = x_shift(value, 1)
-        shifted[pl.ds(base, own), 6] = x_shift(value, -1)
+        put(base, 0, value)
+        put(base, 5, x_shift(value, 1))
+        put(base, 6, x_shift(value, -1))
 
         def edge_pieces(ref, starts, per, wanted, unit, here):
             pieces = []
@@ -217,25 +241,25 @@
 
         low = edge_pieces(ylo, y_starts, y_per, 0, depth, has[0])
         high = edge_pieces(yhi, y_starts, y_per, rows - 1, depth, has[1])
-        shifted[pl.ds(base, own), 1] = jnp.where(row == 0, low, turn(value, depth, 1))
-        shifted[pl.ds(base, own), 2] = jnp.where(row == rows - 1, high, turn(value, -depth, 1))
+        put(base, 1, jnp.where(row == 0, low, turn(value, depth, 1)))
+        put(base, 2, jnp.where(row == rows - 1, high, turn(value, -depth, 1)))
         near = edge_pieces(zlo, z_starts, z_per, 0, 1, has[2])
         far = edge_pieces(zhi, z_starts, z_per, depth - 1, 1, has[3])
-        shifted[pl.ds(base, own), 3] = jnp.where(deep == 0, near, turn(value, 1, 1))
-        shifted[pl.ds(base, own), 4] = jnp.where(deep == depth - 1, far, turn(value, -1, 1))
+        put(base, 3, jnp.where(deep == 0, near, turn(value, 1, 1)))
+        put(base, 4, jnp.where(deep == depth - 1, far, turn(value, -1, 1)))
         for a in range(ACCS):
-            acc[a, pl.ds(base, own)] = jnp.zeros_like(value)
+            acc[a, pl.ds(pl.multiple_of(base * lines, lines), own * lines), :] = jnp.zeros(
+                (own * lines, lanes), jnp.float32)
+
+    def tiles(ref, offset, index):
+        return ref[pl.ds(pl.multiple_of(offset, lines) + index * lines, lines), :]
 
     def add_row(p, a):
-        target = slots[couple[p]]
-        source = slots[couple[pairs + p]]
-        term = couple[2 * pairs + p]
-        image = faces[term, 0] * shifted[source, 0]
-        first = faces[term, 1] * shifted[source, 1] + faces[term, 2] * shifted[source, 2]
-        second = faces[term, 3] * shifted[source, 3] + faces[term, 4] * shifted[source, 4]
-        third = faces[term, 5] * shifted[source, 5] + faces[term, 6] * shifted[source, 6]
-        image = (image - first) - (second + third)
-        acc[a, target] = acc[a, target] + weight[p] * image
+        term, source, target = term_off[p], from_off[p], to_off[p]
+        part = [tiles(faces, term, m) * tiles(shifted, source, m) for m in range(7)]
+        image = (part[0] - (part[1] + part[2])) - ((part[3] + part[4]) + (part[5] + part[6]))
+        here = pl.ds(pl.multiple_of(target, lines), lines)
+        acc[a, here, :] = acc[a, here, :] + weight[p] * image
 
     whole = pairs // UNROLL
 
@@ -249,11 +273,22 @@
 
     @pl.loop(0, n)
     def _(source):
-        base = source * own
-        result = acc[0, pl.ds(base, own)]
+        here = pl.ds(pl.multiple_of(source * own * lines, lines), own * lines)
+        result = acc[0, here, :]
         for a in range(1, ACCS):
-            result = result + acc[a, pl.ds(base, own)]
+            result = result + acc[a, here, :]
         out[source] = result
+
+
+def store_kernel(source, out, held, into, back):
+    count = source.shape[0]
+    for i in range(count):
+        pltpu.make_async_copy(source.at[i], held.at[i], into.at[i]).start()
+    for i in range(count):
+        pltpu.make_async_copy(source.at[i], held.at[i], into.at[i]).wait()
+        pltpu.make_async_copy(held.at[i], out.at[i], back.at[i]).start()
+    for i in range(count):
+        pltpu.make_async_copy(held.at[i], out.at[i], back.at[i]).wait()
 
 
 def collect_kernel(n, result, out, own_sem, send_sem, recv_sem):
@@ -287,6 +322,7 @@
     f32 = jnp.float32
     vmem = pl.BlockSpec(memory_space=pltpu.VMEM)
     smem = pl.BlockSpec(memory_space=pltpu.SMEM)
+    anywhere = pl.BlockSpec(memory_space=pl.ANY)
     dma = pltpu.SemaphoreType.DMA
 
     coef = jnp.concatenate([mean_coeff[None], random_coeff], axis=0)
@@ -295,23 +331,24 @@
     terms = coef.shape[0]
     coef = coef.reshape(terms, (rows + 2) * depth, across)
 
-    degree = coupling[:, 3].astype(f32)
-    raw = (degree + 1.0) / jnp.sqrt((2.0 * degree + 1.0) * (2.0 * degree + 3.0))
-    weight = jnp.where(coupling[:, 2] == 0, jnp.ones_like(raw), raw)
-    pairs = coupling.shape[0]
-    couple = coupling[:, :3].T.reshape(-1)
+    degree = jnp.arange(mode_slots.shape[0], dtype=jnp.int32).astype(f32)
+    table = (degree + 1.0) / jnp.sqrt((2.0 * degree + 1.0) * (2.0 * degree + 3.0))
+    couple = coupling.T
+    pairs = couple.shape[1]
 
     y_per, _ = groups(own, rows)
     z_per, _ = groups(own, depth)
     block = jax.ShapeDtypeStruct((n, own, lines, across), f32)
     y_pack = jax.ShapeDtypeStruct((n, y_per, lines, across), f32)
     z_pack = jax.ShapeDtypeStruct((n, z_per, lines, across), f32)
+    offsets = jax.ShapeDtypeStruct((pairs,), jnp.int32)
     coef_like = jax.ShapeDtypeStruct(coef.shape, f32)
     spread = pl.pallas_call(
         functools.partial(spread_kernel, n, g, rows, depth),
-        out_shape=(block, y_pack, y_pack, z_pack, z_pack, coef_like, coef_like),
-        in_specs=[vmem, vmem],
-        out_specs=[vmem] * 7,
+        out_shape=(block, y_pack, y_pack, z_pack, z_pack, coef_like, coef_like,
+                   offsets, offsets, offsets, jax.ShapeDtypeStruct((pairs,), f32)),
+        in_specs=[smem, smem, smem, anywhere, vmem],
+        out_specs=[vmem] * 7 + [smem] * 4,
         scratch_shapes=[
             pltpu.VMEM(y_pack.shape, f32), pltpu.VMEM(y_pack.shape, f32),
             pltpu.VMEM(z_pack.shape, f32), pltpu.VMEM(z_pack.shape, f32),
@@ -320,21 +357,22 @@
         compiler_params=pltpu.CompilerParams(collective_id=0, has_side_effects=True),
         name="spread",
     )
-    main, ylo, yhi, zlo, zhi, clo, chi = spread(fields.reshape(own, n, lines, across), coef)
+    received = spread(couple, mode_slots, table, fields.reshape(own, n, lines, across), coef)
+    main, ylo, yhi, zlo, zhi, clo, chi, to_off, from_off, term_off, weight = received
 
     mix = pl.pallas_call(
         functools.partial(mix_kernel, n, g, rows, depth, pairs),
-        out_shape=block,
-        in_specs=[smem, smem, smem] + [vmem] * 8,
+        out_shape=jax.ShapeDtypeStruct((n, own * lines, across), f32),
+        in_specs=[smem] * 4 + [vmem] * 8,
         out_specs=vmem,
         scratch_shapes=[
-            pltpu.VMEM((n * own, 7, lines, across), f32),
-            pltpu.VMEM((terms, 7, lines, across), f32),
-            pltpu.VMEM((ACCS, n * own, lines, across), f32),
+            pltpu.VMEM((n * own * 7 * lines, across), f32),
+            pltpu.VMEM((terms * 7 * lines, across), f32),
+            pltpu.VMEM((ACCS, n * own * lines, across), f32),
         ],
         name="mix",
     )
-    result = mix(couple, weight, mode_slots, main, ylo, yhi, zlo, zhi, coef, clo, chi)
+    result = mix(to_off, from_off, term_off, weight, main, ylo, yhi, zlo, zhi, coef, clo, chi)
 
     collect = pl.pallas_call(
         functools.partial(collect_kernel, n),
@@ -345,7 +383,16 @@
         compiler_params=pltpu.CompilerParams(collective_id=1, has_side_effects=True),
         name="collect",
     )
-    return collect(result).reshape(fields.shape)
+    local = (own, n, lines, across)
+    store = pl.pallas_call(
+        store_kernel,
+        out_shape=jax.ShapeDtypeStruct(local, f32),
+        in_specs=[anywhere],
+        out_specs=anywhere,
+        scratch_shapes=[pltpu.VMEM(local, f32), dma((own,)), dma((own,))],
+        name="store",
+    )
+    return store(collect(result.reshape(block.shape))).reshape(fields.shape)
 
 
 def solution(mesh):

time: 97.8 us -> 97 us (level)
  the two profiles are of different devices: /device:TPU:9 before, /device:TPU:0 now
where the time goes in v1:
time: 97 us; the launch traced here: 96.6 us
  Pallas kernels  94.4 us (97%)
  other arithmetic  1.45 us (1%)
    pallas_call x1, Pallas kernels, body(): spread(couple, mode_slots, table, fields.reshape(own, n, lines, across),...  42.5 us
    pallas_call x2, Pallas kernels, body(): return store(collect(result.reshape(block.shape))).reshape(fields.shape)  36.9 us
    pallas_call x1, Pallas kernels, body(): mix(to_off, from_off, term_off, weight, main, ylo, yhi, zlo, zhi, coef, c...  15 us

profile of v1, /device:TPU:0, one launch (start us, length us, event | category | flops | bytes accessed | tf_op | source)
XLA Modules:
  0.0 96.6 jit_solution(13957759502809001807)
XLA Ops:
  0.0 0.6 rsqrt_multiply_fusion.table
  0.6 0.9 fusion.1
  1.5 0.7 reshape.13.coef
  2.1 42.5 %spread.1 = (f32[16,18,8,128]{3,2,1,0:T(8,128)}, f32[16,5,8,128]{3,2,1,0:T(8,128)}, f32[16,5,8,128]{3,2,1,0:T(8,128)}, f32[16,9,8,128]{3,2,1,0:T(8,128)}, f32[16...) custom-call(s32[4,1606]{1,0:T(4,128)} %bitcast.8, ...), custom_call_target="tpu_custom_call" | custom-call | tf_op jit(solution)/shard_map/spread/pallas_call | solution.py:360
  44.6 15.0 %mix.1 = f32[16,144,128]{2,1,0:T(8,128)} custom-call(s32[1606]{0:T(1024)} %get-tuple-element.16.to_off, s32[1606]{0:T(1024)} %get-tuple-element.17.from_off, s32[1606]{0:T(1024)} %get-tuple-element.18.term_off, f32[1606]{0:T(1024)} %get-tuple-element.19.weight, f32[16,18,8,128]{3,2,1,0:T(8,128)} %get-tuple-element.20.main, ...), custom_call_target="tpu_custom_call" | custom-call | tf_op jit(solution)/shard_map/mix/pallas_call | solution.py:375
  59.6 34.7 %collect.1.source = f32[18,16,8,128]{3,2,1,0:T(8,128)} custom-call(f32[16,18,8,128]{3,2,1,0:T(8,128)} %bitcast.5), custom_call_target="tpu_custom_call" | custom-call | tf_op jit(solution)/shard_map/collect/pallas_call | solution.py:395
  94.3 2.2 %store.1 = f32[18,16,8,128]{3,2,1,0:T(8,128)} custom-call(f32[18,16,8,128]{3,2,1,0:T(8,128)} %collect.1.source), custom_call_target="tpu_custom_call" | custom-call | tf_op jit(solution)/shard_map/store/pallas_call | solution.py:395

commit v2 on v1

--- a/solution.py
+++ b/solution.py
@@ -7,7 +7,7 @@
 from jax.experimental.pallas import tpu as pltpu
 from jax.sharding import PartitionSpec as P
 
-ACCS = 4
+ACCS = 2
 UNROLL = 22
 
 
@@ -21,8 +21,20 @@
     return jnp.concatenate([low, high], axis=axis)
 
 
-def send_order(count):
-    return sorted(range(1, count), key=lambda d: (min(d, count - d), d))
+def step_plan(count):
+    plane = max(p for p in range(1, count + 1) if count % p == 0 and p * p <= count)
+    planes = count // plane
+    far = sorted(range(1, planes), key=lambda d: (abs(d - planes // 2), d))
+    near = [(0, j) for j in range(1, plane)]
+    away = [(d, j) for d in far for j in range(plane)]
+    return away + near, near + away, plane
+
+
+def partner(me, step, count, plane, sign):
+    planes = count // plane
+    outer = lax.rem(me // plane + planes + sign * step[0], planes)
+    inner = lax.rem(lax.rem(me, plane) + plane + sign * step[1], plane)
+    return outer * plane + inner
 
 
 def groups(own, parts):
@@ -50,8 +62,8 @@
 
 
 def spread_kernel(n, g, rows, depth, couple, slots, table, fields, coef,
-                  main, ylo, yhi, zlo, zhi, clo, chi, to_off, from_off, term_off, weight,
-                  ylo_out, yhi_out, zlo_out, zhi_out,
+                  main_out, ylo, yhi, zlo, zhi, clo, chi, to_off, from_off, term_off, weight,
+                  main, ylo_out, yhi_out, zlo_out, zhi_out, out_sem,
                   own_sem, send_sem, recv_sem, halo_send, halo_recv, coef_send, coef_recv):
     me, layer = lax.axis_index("modes"), lax.axis_index("gz")
     own = fields.shape[0]
@@ -63,11 +75,14 @@
     landing = (yhi, ylo, zhi, zlo)
     barrier_with_peers(n, g)
 
+    sends, waits, plane = step_plan(n)
+
     def block_copy(step):
-        target = lax.rem(me + step, n)
+        target = partner(me, step, n, plane, 1)
+        slot = step[0] * plane + step[1]
         return pltpu.make_async_remote_copy(
             src_ref=fields.at[:, target], dst_ref=main.at[me],
-            send_sem=send_sem.at[step], recv_sem=recv_sem.at[step],
+            send_sem=send_sem.at[slot], recv_sem=recv_sem.at[slot],
             device_id=(target, layer), device_id_type=mesh_id)
 
     def coef_copy(side):
@@ -82,8 +97,7 @@
             send_sem=halo_send.at[side, source], recv_sem=halo_recv.at[side, source],
             device_id=to[side], device_id_type=mesh_id)
 
-    order = send_order(n)
-    for step in order:
+    for step in sends:
         block_copy(step).start()
     mine = pltpu.make_async_copy(fields.at[:, me], main.at[me], own_sem)
     mine.start()
@@ -122,6 +136,9 @@
                 tile = part if tile is None else jnp.where(line % depth == j, part, tile)
             out[source] = tile
 
+    def keep(source):
+        return pltpu.make_async_copy(main.at[source], main_out.at[source], out_sem.at[source])
+
     def send_halo(source):
         for side in range(4):
             @pl.when(has[side])
@@ -130,18 +147,25 @@
 
     decode(0)
     mine.wait()
+    keep(me).start()
     pack(me)
     previous = me
-    for part, step in enumerate(order):
-        source = lax.rem(me + n - step, n)
+    for part, step in enumerate(waits):
+        source = partner(me, step, n, plane, -1)
         block_copy(step).wait_recv()
+        keep(source).start()
         send_halo(previous)
         pack(source)
         decode(part + 1)
         previous = source
-    for step in order:
+    for step in sends:
         block_copy(step).wait_send()
     send_halo(previous)
+
+    @pl.loop(0, n)
+    def _(source):
+        keep(source).wait()
+
     for side in range(4):
         @pl.when(has[side])
         def _():
@@ -166,8 +190,20 @@
             coef_copy(side).wait_recv()
 
 
-def mix_kernel(n, g, rows, depth, pairs, to_off, from_off, term_off, weight, main, ylo, yhi, zlo, zhi,
-               coef, clo, chi, out, shifted, faces, acc):
+def mix_kernel(n, g, rows, depth, pairs, to_off, from_off, term_off, weight, *rest):
+    given, (coef, clo, chi, out), rest = rest[:5], rest[5:9], rest[9:]
+    held, (sem, shifted, faces), acc = rest[:5], rest[5:8], rest[8:]
+    main, ylo, yhi, zlo, zhi = held
+
+    def fetch(i, source):
+        return pltpu.make_async_copy(
+            given[i].at[source], held[i].at[source], sem.at[i, source])
+
+    @pl.loop(0, n)
+    def _(source):
+        for i in range(5):
+            fetch(i, source).start()
+
     me, layer = lax.axis_index("modes"), lax.axis_index("gz")
     own = main.shape[1]
     lines = rows * depth
@@ -224,6 +260,8 @@
 
     @pl.loop(0, n)
     def _(source):
+        for i in range(5):
+            fetch(i, source).wait()
         base = source * own
         value = main[source]
         put(base, 0, value)
@@ -248,7 +286,7 @@
         put(base, 3, jnp.where(deep == 0, near, turn(value, 1, 1)))
         put(base, 4, jnp.where(deep == depth - 1, far, turn(value, -1, 1)))
         for a in range(ACCS):
-            acc[a, pl.ds(pl.multiple_of(base * lines, lines), own * lines), :] = jnp.zeros(
+            acc[a][pl.ds(pl.multiple_of(base * lines, lines), own * lines), :] = jnp.zeros(
                 (own * lines, lanes), jnp.float32)
 
     def tiles(ref, offset, index):
@@ -259,7 +297,7 @@
         part = [tiles(faces, term, m) * tiles(shifted, source, m) for m in range(7)]
         image = (part[0] - (part[1] + part[2])) - ((part[3] + part[4]) + (part[5] + part[6]))
         here = pl.ds(pl.multiple_of(target, lines), lines)
-        acc[a, here, :] = acc[a, here, :] + weight[p] * image
+        acc[a][here, :] = acc[a][here, :] + weight[p] * image
 
     whole = pairs // UNROLL
 
@@ -274,9 +312,9 @@
     @pl.loop(0, n)
     def _(source):
         here = pl.ds(pl.multiple_of(source * own * lines, lines), own * lines)
-        result = acc[0, here, :]
+        result = acc[0][here, :]
         for a in range(1, ACCS):
-            result = result + acc[a, here, :]
+            result = result + acc[a][here, :]
         out[source] = result
 
 
@@ -295,22 +333,24 @@
     me, layer = lax.axis_index("modes"), lax.axis_index("gz")
     barrier_with_peers(n, 1)
 
+    sends, waits, plane = step_plan(n)
+
     def block_copy(step):
-        target = lax.rem(me + step, n)
+        target = partner(me, step, n, plane, 1)
+        slot = step[0] * plane + step[1]
         return pltpu.make_async_remote_copy(
             src_ref=result.at[target], dst_ref=out.at[:, me],
-            send_sem=send_sem.at[step], recv_sem=recv_sem.at[step],
+            send_sem=send_sem.at[slot], recv_sem=recv_sem.at[slot],
             device_id=(target, layer), device_id_type=pl.DeviceIdType.MESH)
 
-    order = send_order(n)
-    for step in order:
+    for step in sends:
         block_copy(step).start()
     mine = pltpu.make_async_copy(result.at[me], out.at[:, me], own_sem)
     mine.start()
     mine.wait()
-    for step in order:
+    for step in waits:
         block_copy(step).wait_recv()
-    for step in order:
+    for step in waits:
         block_copy(step).wait_send()
 
 
@@ -348,10 +388,11 @@
         out_shape=(block, y_pack, y_pack, z_pack, z_pack, coef_like, coef_like,
                    offsets, offsets, offsets, jax.ShapeDtypeStruct((pairs,), f32)),
         in_specs=[smem, smem, smem, anywhere, vmem],
-        out_specs=[vmem] * 7 + [smem] * 4,
+        out_specs=[anywhere] * 7 + [smem] * 4,
         scratch_shapes=[
+            pltpu.VMEM(block.shape, f32),
             pltpu.VMEM(y_pack.shape, f32), pltpu.VMEM(y_pack.shape, f32),
-            pltpu.VMEM(z_pack.shape, f32), pltpu.VMEM(z_pack.shape, f32),
+            pltpu.VMEM(z_pack.shape, f32), pltpu.VMEM(z_pack.shape, f32), dma((n,)),
             dma, dma((n,)), dma((n,)), dma((4, n)), dma((4, n)), dma((2,)), dma((2,)),
         ],
         compiler_params=pltpu.CompilerParams(collective_id=0, has_side_effects=True),
@@ -363,13 +404,13 @@
     mix = pl.pallas_call(
         functools.partial(mix_kernel, n, g, rows, depth, pairs),
         out_shape=jax.ShapeDtypeStruct((n, own * lines, across), f32),
-        in_specs=[smem] * 4 + [vmem] * 8,
+        in_specs=[smem] * 4 + [anywhere] * 5 + [vmem] * 3,
         out_specs=vmem,
-        scratch_shapes=[
+        scratch_shapes=[pltpu.VMEM(a.shape, f32) for a in received[:5]] + [
+            dma((5, n)),
             pltpu.VMEM((n * own * 7 * lines, across), f32),
             pltpu.VMEM((terms * 7 * lines, across), f32),
-            pltpu.VMEM((ACCS, n * own * lines, across), f32),
-        ],
+        ] + [pltpu.VMEM((n * own * lines, across), f32)] * ACCS,
         name="mix",
     )
     result = mix(to_off, from_off, term_off, weight, main, ylo, yhi, zlo, zhi, coef, clo, chi)
@@ -378,7 +419,7 @@
         functools.partial(collect_kernel, n),
         out_shape=jax.ShapeDtypeStruct((own, n, lines, across), f32),
         in_specs=[vmem],
-        out_specs=vmem,
+        out_specs=anywhere,
         scratch_shapes=[dma, dma((n,)), dma((n,))],
         compiler_params=pltpu.CompilerParams(collective_id=1, has_side_effects=True),
         name="collect",

time: 97 us -> 94.1 us (0.970)
  the two profiles are of different devices: /device:TPU:0 before, /device:TPU:9 now
where the time goes in v2:
time: 94.1 us; the launch traced here: 93.6 us
  Pallas kernels  91.4 us (97%)
  other arithmetic  1.48 us (2%)
    pallas_call x1, Pallas kernels, body(): spread(couple, mode_slots, table, fields.reshape(own, n, lines, across),...  39.7 us
    pallas_call x2, Pallas kernels, body(): return store(collect(result.reshape(block.shape))).reshape(fields.shape)  38.8 us
    pallas_call x1, Pallas kernels, body(): mix(to_off, from_off, term_off, weight, main, ylo, yhi, zlo, zhi, coef, c...  12.9 us

profile of v2, /device:TPU:9, one launch (start us, length us, event | category | flops | bytes accessed | tf_op | source)
XLA Modules:
  0.0 93.6 jit_solution(16476194600739055639)
XLA Ops:
  0.0 0.6 rsqrt_multiply_fusion.table
  0.6 0.9 fusion.1
  1.5 0.7 reshape.13.coef.rest_5_
  2.2 39.7 %spread.1 = (f32[16,18,8,128]{3,2,1,0:T(8,128)}, f32[16,5,8,128]{3,2,1,0:T(8,128)}, f32[16,5,8,128]{3,2,1,0:T(8,128)}, f32[16,9,8,128]{3,2,1,0:T(8,128)}, f32[16...) custom-call(s32[4,1606]{1,0:T(4,128)} %bitcast.8, ...), custom_call_target="tpu_custom_call" | custom-call | tf_op jit(solution)/shard_map/spread/pallas_call | solution.py:401
  41.9 12.9 %mix.1 = f32[16,144,128]{2,1,0:T(8,128)} custom-call(s32[1606]{0:T(1024)} %get-tuple-element.16.to_off, s32[1606]{0:T(1024)} %get-tuple-element.17.from_off, s32[1606]{0:T(1024)} %get-tuple-element.18.term_off, f32[1606]{0:T(1024)} %get-tuple-element.19.weight, f32[16,18,8,128]{3,2,1,0:T(8,128)} %get-tuple-element.20.rest_0_, ...), custom_call_target="tpu_custom_call" | custom-call | tf_op jit(solution)/shard_map/mix/pallas_call | solution.py:416
  54.8 36.5 %collect.1.source = f32[18,16,8,128]{3,2,1,0:T(8,128)} custom-call(f32[16,18,8,128]{3,2,1,0:T(8,128)} %bitcast.5), custom_call_target="tpu_custom_call" | custom-call | tf_op jit(solution)/shard_map/collect/pallas_call | solution.py:436
  91.3 2.2 %store.1 = f32[18,16,8,128]{3,2,1,0:T(8,128)} custom-call(f32[18,16,8,128]{3,2,1,0:T(8,128)} %collect.1.source), custom_call_target="tpu_custom_call" | custom-call | tf_op jit(solution)/shard_map/store/pallas_call | solution.py:436

commit v3 on v2

--- a/solution.py
+++ b/solution.py
@@ -8,7 +8,7 @@
 from jax.sharding import PartitionSpec as P
 
 ACCS = 2
-UNROLL = 22
+UNROLL = 73
 
 
 def turn(value, shift, axis):
@@ -75,7 +75,8 @@
     landing = (yhi, ylo, zhi, zlo)
     barrier_with_peers(n, g)
 
-    sends, waits, plane = step_plan(n)
+    _, sends, plane = step_plan(n)
+    waits = sends
 
     def block_copy(step):
         target = partner(me, step, n, plane, 1)

time: 94.1 us -> 93.8 us (level)
  no operation moved by 1% of the time
where the time goes in v3:
time: 93.8 us; the launch traced here: 93.4 us
  Pallas kernels  91.2 us (97%)
  other arithmetic  1.48 us (2%)
    pallas_call x1, Pallas kernels, body(): spread(couple, mode_slots, table, fields.reshape(own, n, lines, across),...  39.7 us
    pallas_call x2, Pallas kernels, body(): return store(collect(result.reshape(block.shape))).reshape(fields.shape)  38.8 us
    pallas_call x1, Pallas kernels, body(): mix(to_off, from_off, term_off, weight, main, ylo, yhi, zlo, zhi, coef, c...  12.7 us

profile of v3, /device:TPU:9, one launch (start us, length us, event | category | flops | bytes accessed | tf_op | source)
XLA Modules:
  0.0 93.4 jit_solution(1003265739917226482)
XLA Ops:
  0.0 0.6 rsqrt_multiply_fusion.table
  0.6 0.9 fusion.1
  1.5 0.7 reshape.13.coef.rest_5_
  2.2 39.7 %spread.1 = (f32[16,18,8,128]{3,2,1,0:T(8,128)}, f32[16,5,8,128]{3,2,1,0:T(8,128)}, f32[16,5,8,128]{3,2,1,0:T(8,128)}, f32[16,9,8,128]{3,2,1,0:T(8,128)}, f32[16...) custom-call(s32[4,1606]{1,0:T(4,128)} %bitcast.8, ...), custom_call_target="tpu_custom_call" | custom-call | tf_op jit(solution)/shard_map/spread/pallas_call | solution.py:402
  41.9 12.7 %mix.1 = f32[16,144,128]{2,1,0:T(8,128)} custom-call(s32[1606]{0:T(1024)} %get-tuple-element.16.to_off, s32[1606]{0:T(1024)} %get-tuple-element.17.from_off, s32[1606]{0:T(1024)} %get-tuple-element.18.term_off, f32[1606]{0:T(1024)} %get-tuple-element.19.weight, f32[16,18,8,128]{3,2,1,0:T(8,128)} %get-tuple-element.20.rest_0_, ...), custom_call_target="tpu_custom_call" | custom-call | tf_op jit(solution)/shard_map/mix/pallas_call | solution.py:417
  54.6 36.5 %collect.1.source = f32[18,16,8,128]{3,2,1,0:T(8,128)} custom-call(f32[16,18,8,128]{3,2,1,0:T(8,128)} %bitcast.5), custom_call_target="tpu_custom_call" | custom-call | tf_op jit(solution)/shard_map/collect/pallas_call | solution.py:437
  91.1 2.2 %store.1 = f32[18,16,8,128]{3,2,1,0:T(8,128)} custom-call(f32[18,16,8,128]{3,2,1,0:T(8,128)} %collect.1.source), custom_call_target="tpu_custom_call" | custom-call | tf_op jit(solution)/shard_map/store/pallas_call | solution.py:437

commit v4 on v3

--- a/solution.py
+++ b/solution.py
@@ -75,12 +75,11 @@
     landing = (yhi, ylo, zhi, zlo)
     barrier_with_peers(n, g)
 
-    _, sends, plane = step_plan(n)
+    sends = sorted(range(1, n), key=lambda d: (abs(d - n // 2), d))
     waits = sends
 
-    def block_copy(step):
-        target = partner(me, step, n, plane, 1)
-        slot = step[0] * plane + step[1]
+    def block_copy(slot):
+        target = lax.rem(me + slot, n)
         return pltpu.make_async_remote_copy(
             src_ref=fields.at[:, target], dst_ref=main.at[me],
             send_sem=send_sem.at[slot], recv_sem=recv_sem.at[slot],
@@ -152,7 +151,7 @@
     pack(me)
     previous = me
     for part, step in enumerate(waits):
-        source = partner(me, step, n, plane, -1)
+        source = lax.rem(me + n - step, n)
         block_copy(step).wait_recv()
         keep(source).start()
         send_halo(previous)

time: 93.8 us -> 97.8 us (1.043)
  Pallas kernels: 91.2 us -> 95.2 us
    pallas_call x1, Pallas kernels: 39.7 us -> 48.5 us  [body(): spread(couple, mode_slots, table, fields.reshape(own, n, lines, across),...]
    pallas_call x2, Pallas kernels: 38.8 us -> 34 us  [body(): return store(collect(result.reshape(block.shape))).reshape(fields.shape)]
where the time goes in v4:
time: 97.8 us; the launch traced here: 97.4 us
  Pallas kernels  95.2 us (97%)
  other arithmetic  1.48 us (2%)
    pallas_call x1, Pallas kernels, body(): spread(couple, mode_slots, table, fields.reshape(own, n, lines, across),...  48.5 us
    pallas_call x2, Pallas kernels, body(): return store(collect(result.reshape(block.shape))).reshape(fields.shape)  34 us
    pallas_call x1, Pallas kernels, body(): mix(to_off, from_off, term_off, weight, main, ylo, yhi, zlo, zhi, coef, c...  12.7 us

profile of v4, /device:TPU:9, one launch (start us, length us, event | category | flops | bytes accessed | tf_op | source)
XLA Modules:
  0.0 97.4 jit_solution(13625686082561228847)
XLA Ops:
  0.0 0.6 rsqrt_multiply_fusion.table
  0.6 0.9 fusion.1
  1.5 0.7 reshape.13.coef.rest_5_
  2.2 48.5 %spread.1 = (f32[16,18,8,128]{3,2,1,0:T(8,128)}, f32[16,5,8,128]{3,2,1,0:T(8,128)}, f32[16,5,8,128]{3,2,1,0:T(8,128)}, f32[16,9,8,128]{3,2,1,0:T(8,128)}, f32[16...) custom-call(s32[4,1606]{1,0:T(4,128)} %bitcast.8, ...), custom_call_target="tpu_custom_call" | custom-call | tf_op jit(solution)/shard_map/spread/pallas_call | solution.py:401
  50.7 12.7 %mix.1 = f32[16,144,128]{2,1,0:T(8,128)} custom-call(s32[1606]{0:T(1024)} %get-tuple-element.16.to_off, s32[1606]{0:T(1024)} %get-tuple-element.17.from_off, s32[1606]{0:T(1024)} %get-tuple-element.18.term_off, f32[1606]{0:T(1024)} %get-tuple-element.19.weight, f32[16,18,8,128]{3,2,1,0:T(8,128)} %get-tuple-element.20.rest_0_, ...), custom_call_target="tpu_custom_call" | custom-call | tf_op jit(solution)/shard_map/mix/pallas_call | solution.py:416
  63.4 31.7 %collect.1.source = f32[18,16,8,128]{3,2,1,0:T(8,128)} custom-call(f32[16,18,8,128]{3,2,1,0:T(8,128)} %bitcast.5), custom_call_target="tpu_custom_call" | custom-call | tf_op jit(solution)/shard_map/collect/pallas_call | solution.py:436
  95.1 2.2 %store.1 = f32[18,16,8,128]{3,2,1,0:T(8,128)} custom-call(f32[18,16,8,128]{3,2,1,0:T(8,128)} %collect.1.source), custom_call_target="tpu_custom_call" | custom-call | tf_op jit(solution)/shard_map/store/pallas_call | solution.py:436
